TPU v7x, 32 devices: a whole 2x2x4 slice. The times are simulated.
32 devices in a mesh: row: 8 (over z, y), col: 4 (over x, core).
Axes of the slice: x: 2, y: 2, z: 4, core: 2. Of those that a mesh axis runs over, the one named last changes fastest.
Arguments:
- tile_u: bfloat16 [3, 8, 2, 4, 512, 128], P(None, 'row', None, 'col'), may hold values from -6 to 6
- tile_v: bfloat16 [3, 8, 2, 4, 512, 128], P(None, 'row', None, 'col'), may hold values from -6 to 6
- tile_ranks: int32 [3, 8, 2, 4], P(None, 'row', None, 'col'), may hold values from 16 to 128
- lower_inverse: bfloat16 [2, 512, 512], replicated, as said below
- upper_inverse: bfloat16 [2, 512, 512], replicated, as said below
- row_order: int32 [2, 512], replicated, may hold values from 0 to 511, each once within a row
- sketch: bfloat16 [512, 128], replicated, may hold values from -0.25 to 0.25
Outputs:
- new_u: bfloat16 [3, 8, 2, 4, 512, 128], P(None, 'row', None, 'col')
- new_v: bfloat16 [3, 8, 2, 4, 512, 128], P(None, 'row', None, 'col')
Inputs may be any that keep to these rules, and one draw needn't show every extreme that they name: Each row of row_order names every number of 0 to 511 once. Each lower_inverse[k] is lower triangular with a unit diagonal. Each upper_inverse[k] is upper triangular with a positive diagonal.
All inputs are finite; a program needn't handle non-finite values.
Results may differ from a plain program's by a relative error of at most 0.03.
Values may be sent and summed in bfloat16 or wider, within the bound.
A program may use at most 64 MiB of HBM per device.

v0:
```python
import jax
import jax.numpy as jnp
from jax import lax
from jax.sharding import PartitionSpec as P

PANELS = 2


HIGHEST = lax.Precision.HIGHEST


def from_root(array, axis, root):
    mine = lax.axis_index(axis) == root
    return lax.psum(jnp.where(mine, array, jnp.zeros_like(array)), axis)


def compress(tile_uf, tile_vf, left_u, coupling, top_v, keep_cols, sketch):
    rank_width = tile_uf.shape[-1]
    tile_size = tile_uf.shape[-2]
    product = jnp.einsum("...br,...rs->...bs", left_u, coupling, preferred_element_type=jnp.float32)
    update = (product * rank_width ** (-0.5)).astype(jnp.bfloat16)
    stacked_left = jnp.concatenate([tile_uf, -update], axis=-1)
    stacked_right = jnp.concatenate([tile_vf, top_v], axis=-1)
    probe_mat = jnp.einsum(
        "...bt,br->...tr", stacked_right, sketch, preferred_element_type=jnp.float32
    )
    left_wide = stacked_left.astype(jnp.float32)
    sample = (
        jnp.einsum("...bt,...tr->...br", left_wide, probe_mat, precision=HIGHEST)
        * keep_cols[..., None, :]
    )
    gram_matrix = jnp.einsum("...br,...bs->...rs", sample, sample, precision=HIGHEST)
    gram_matrix = gram_matrix + (1.0 - keep_cols)[..., :, None] * jnp.eye(
        rank_width, dtype=jnp.float32
    )
    factor = jnp.linalg.cholesky(gram_matrix)
    solved = lax.linalg.triangular_solve(
        factor, jnp.swapaxes(sample, -1, -2), left_side=True, lower=True
    )
    new_basis = jnp.swapaxes(solved, -1, -2)
    weights_q = jnp.einsum("...bt,...br->...tr", left_wide, new_basis, precision=HIGHEST)
    fresh_v = jnp.einsum(
        "...bt,...tr->...br", stacked_right.astype(jnp.float32), weights_q, precision=HIGHEST
    )
    return (
        (new_basis * tile_size**0.5).astype(jnp.bfloat16),
        (fresh_v * tile_size ** (-0.5)).astype(jnp.bfloat16),
    )


def on_device(tile_u, tile_v, tile_ranks, lower_inverse, upper_inverse, row_order, sketch):
    row_tiles, col_tiles = (tile_u.shape[0], tile_u.shape[2])
    tile_size, rank_width = (tile_u.shape[4], tile_u.shape[5])
    shape_four = (row_tiles, col_tiles, tile_size, rank_width)
    tile_rank = tile_ranks.reshape(row_tiles, col_tiles)
    keep_flags_mask = jnp.arange(rank_width, dtype=jnp.int32)[None, None, :] < tile_rank[:, :, None]
    keep_cols = keep_flags_mask.astype(jnp.float32)
    keep_half = keep_flags_mask.astype(jnp.bfloat16)[:, :, None, :]
    factor_left_bases = tile_u.reshape(shape_four) * keep_half
    factors_v = tile_v.reshape(shape_four) * keep_half
    row_place = lax.axis_index("row")
    col_place = lax.axis_index("col")
    global_rows = jnp.arange(row_tiles, dtype=jnp.int32) * lax.axis_size("row") + row_place
    global_cols = jnp.arange(col_tiles, dtype=jnp.int32) * lax.axis_size("col") + col_place

    def prepare(panel, factor_left_bases, factors_v):
        permuted = jnp.take(factor_left_bases[0], row_order[panel], axis=1)
        turned_u = jnp.einsum(
            "ab,mbr->mar", lower_inverse[panel], permuted, preferred_element_type=jnp.float32
        ).astype(jnp.bfloat16)
        top_u = jnp.where((global_cols > panel)[:, None, None], turned_u, factor_left_bases[0])
        transposed_right_basis = jnp.einsum(
            "ba,lbr->lar", upper_inverse[panel], factors_v[:, 0], preferred_element_type=jnp.float32
        )
        transposed_right_basis = (transposed_right_basis * tile_size**0.5).astype(jnp.bfloat16)
        left_right_basis = jnp.where(
            (global_rows > panel)[:, None, None], transposed_right_basis, factors_v[:, 0]
        )
        factor_left_bases = factor_left_bases.at[0].set(
            jnp.where(row_place == panel, top_u, factor_left_bases[0])
        )
        factors_v = factors_v.at[:, 0].set(
            jnp.where(col_place == panel, left_right_basis, factors_v[:, 0])
        )
        panel_upper_left_basis, panel_top_v = (
            from_root(top_u, "row", panel),
            from_root(factors_v[0], "row", panel),
        )
        panel_left_u, panel_left_right_basis = (
            from_root(factor_left_bases[:, 0], "col", panel),
            from_root(left_right_basis, "col", panel),
        )
        coupling = jnp.einsum(
            "nxu,ixp->niup",
            panel_left_right_basis,
            panel_upper_left_basis,
            preferred_element_type=jnp.float32,
        )
        coupling = (coupling * tile_size ** (-0.5)).astype(jnp.bfloat16)
        return (factor_left_bases, factors_v, panel_left_u, coupling, panel_top_v)

    def refresh(
        panel, block_u, block_v, left_u, coupling, top_v, keep_block, rows_block, cols_block
    ):
        left_full = jnp.broadcast_to(left_u[:, None], block_u.shape)
        top_full = jnp.broadcast_to(top_v[None, :], block_v.shape)
        fresh_u, fresh_v = compress(
            block_u, block_v, left_full, coupling, top_full, keep_block, sketch
        )
        chosen = ((rows_block > panel)[:, None] & (cols_block > panel)[None, :])[:, :, None, None]
        return (jnp.where(chosen, fresh_u, block_u), jnp.where(chosen, fresh_v, block_v))

    prepared = prepare(0, factor_left_bases, factors_v)
    for panel in range(PANELS):
        factor_left_bases, factors_v, left_u, coupling, top_v = prepared
        if panel + 1 < PANELS:
            head_u, head_v = refresh(
                panel,
                factor_left_bases[:1],
                factors_v[:1],
                left_u[:1],
                coupling[:1],
                top_v,
                keep_cols[:1],
                global_rows[:1],
                global_cols,
            )
            lateral_left_basis, side_v = refresh(
                panel,
                factor_left_bases[1:, :1],
                factors_v[1:, :1],
                left_u[1:],
                coupling[1:, :1],
                top_v[:1],
                keep_cols[1:, :1],
                global_rows[1:],
                global_cols[:1],
            )
            factor_left_bases = (
                factor_left_bases.at[:1].set(head_u).at[1:, :1].set(lateral_left_basis)
            )
            factors_v = factors_v.at[:1].set(head_v).at[1:, :1].set(side_v)
            prepared = prepare(panel + 1, factor_left_bases, factors_v)
            factor_left_bases, factors_v = (prepared[0], prepared[1])
            inner_u, inner_v = refresh(
                panel,
                factor_left_bases[1:, 1:],
                factors_v[1:, 1:],
                left_u[1:],
                coupling[1:, 1:],
                top_v[1:],
                keep_cols[1:, 1:],
                global_rows[1:],
                global_cols[1:],
            )
            factor_left_bases = factor_left_bases.at[1:, 1:].set(inner_u)
            factors_v = factors_v.at[1:, 1:].set(inner_v)
            prepared = (factor_left_bases, factors_v) + tuple(prepared[2:])
        else:
            factor_left_bases, factors_v = refresh(
                panel,
                factor_left_bases,
                factors_v,
                left_u,
                coupling,
                top_v,
                keep_cols,
                global_rows,
                global_cols,
            )
    return (factor_left_bases.reshape(tile_u.shape), factors_v.reshape(tile_v.shape))


def solution(mesh):
    in_specs = (
        P(None, "row", None, "col", None, None),
        P(None, "row", None, "col", None, None),
        P(None, "row", None, "col"),
        P(),
        P(),
        P(),
        P(),
    )
    out_specs = (P(None, "row", None, "col", None, None), P(None, "row", None, "col", None, None))
    return jax.shard_map(
        on_device, mesh=mesh, in_specs=in_specs, out_specs=out_specs, check_vma=False
    )
```

profile of v0, /device:TPU:28, one launch (start us, length us, event | category | flops | bytes accessed | tf_op | source)
XLA Modules:
  0.0 548.5 jit_solution(12464353481008873408)
XLA Ops:
  7.2 1.5 copy.185
  8.8 0.7 fusion.117
  11.5 2.1 gather_fusion
  13.6 1.8 fusion.90
  15.4 2.2 broadcast_select_fusion.6
  17.6 0.8 fusion.65
  18.4 1.1 broadcast_select_fusion.4
  19.7 0.8 select_bitcast_fusion.1
  20.7 0.7 slice_bitcast_fusion.5
  21.5 0.7 slice_bitcast_fusion.7
  23.4 0.7 broadcast_subtract_fusion
  24.8 0.7 fusion.136
  26.7 0.7 compare_and_fusion.2
  28.5 0.7 slice_bitcast_fusion.8
  29.3 26.4 %all-reduce.15.cloned.1.call-done = (bf16[3,512,128]{1,2,0:T(8,128)(2,1)}, bf16[3,512,128]{1,2,0:T(8,128)(2,1)}) async-done(((bf16[3,512,128]{1,2,0:T(8,128)(2,1)}, bf16[3,512,128]{1,2,0:T(8,128)(2,1)}), (bf16[3,512,128]{1,2,0:T(8,128)(2,1)}, bf16[3,512,128]{1,2,0:T(8,128)(2,1)})) %all-reduce.15.cloned.1.call-update) | async-done | bytes 786448 | tf_op jit(solution)/shard_map/psum | solution.py:14
  55.7 1.0 slice_bitcast_fusion.11
  56.8 73.4 %all-reduce.11.cloned.1.call-done = (bf16[2,512,128]{1,2,0:T(8,128)(2,1)}, bf16[2,512,128]{1,2,0:T(8,128)(2,1)}) async-done(((bf16[2,512,128]{1,2,0:T(8,128)(2,1)}, bf16[2,512,128]{1,2,0:T(8,128)(2,1)}), (bf16[2,512,128]{1,2,0:T(8,128)(2,1)}, bf16[2,512,128]{1,2,0:T(8,128)(2,1)})) %all-reduce.11.cloned.1.call-update) | async-done | bytes 524304 | tf_op jit(solution)/shard_map/psum | solution.py:14
  130.2 1.5 fusion.34
  131.7 1.9 fusion.21
  134.1 0.7 slice_bitcast_fusion.9
  135.1 0.7 convolution_multiply_fusion.11
  135.8 1.0 fusion.35
  137.0 23.9 %custom-call.20 = f32[1,2,128,128]{3,2,1,0:T(8,128)S(1)} custom-call(f32[1,2,128,128]{3,2,1,0:T(8,128)S(1)} %copy.193), custom_call_target="Cholesky" | custom-call | tf_op jit(solution)/shard_map/jit(cholesky)/cholesky | solution.py:36
  161.2 20.3 %custom-call.21 = f32[1,2,1,128,128]{3,4,2,1,0:T(8,128)} custom-call(f32[1,2,1,128,128]{4,3,2,1,0:T(8,128)S(1)} %select_bitcast_fusion.3), custom_call_target="InvertDiagBlocksLowerTriangular" | custom-call | tf_op jit(solution)/shard_map/triangular_solve | solution.py:37
  181.5 0.9 broadcast_in_dim.170
  182.4 1.3 fusion.62
  183.8 1.7 convolution_multiply_fusion.10
  185.5 2.5 convolution_add_fusion.1
  188.0 1.6 copy.201
  189.7 1.6 fusion.98
  191.3 24.9 %custom-call.26 = f32[2,1,128,128]{3,2,1,0:T(8,128)} custom-call(f32[2,1,128,128]{3,2,1,0:T(8,128)} %fusion.98), custom_call_target="Cholesky" | custom-call | tf_op jit(solution)/shard_map/jit(cholesky)/cholesky | solution.py:36
  216.2 0.9 fusion.105
  217.3 1.6 fusion.108
  218.9 21.2 %custom-call.27 = f32[2,1,1,128,128]{3,4,2,1,0:T(8,128)} custom-call(f32[2,1,1,128,128]{4,3,2,1,0:T(8,128)} %fusion.108), custom_call_target="InvertDiagBlocksLowerTriangular" | custom-call | tf_op jit(solution)/shard_map/triangular_solve/custom-call.4 | solution.py:37
  240.2 2.4 fusion.78
  242.6 1.5 fusion.81
  244.3 2.1 gather_fusion.1
  246.4 1.8 fusion.91
  248.2 2.1 broadcast_select_fusion.5
  250.4 0.8 fusion.64
  253.7 0.7 copy-done.60
  254.4 1.2 bitcast_dynamic-update-slice_fusion
  256.5 0.7 convolution_multiply_fusion.7
  257.2 1.0 convolution_add_fusion
  258.3 0.7 fusion.96
  258.9 24.3 %custom-call.28 = f32[2,1,128,128]{3,2,1,0:T(8,128)S(1)} custom-call(f32[2,1,128,128]{3,2,1,0:T(8,128)} %fusion.96), custom_call_target="Cholesky" | custom-call | tf_op jit(solution)/shard_map/jit(cholesky)/cholesky | solution.py:36
  283.4 0.8 broadcast_select_fusion.2
  284.3 19.9 %custom-call.29 = f32[2,1,1,128,128]{3,4,2,1,0:T(8,128)S(1)} custom-call(f32[2,1,1,128,128]{4,3,2,1,0:T(8,128)S(1)} %fusion.103), custom_call_target="InvertDiagBlocksLowerTriangular" | custom-call | tf_op jit(solution)/shard_map/triangular_solve/custom-call.4 | solution.py:37
  304.2 0.7 fusion.85
  305.0 1.4 fusion.84
  307.5 13.0 %all-reduce.13.cloned.1.call-done = (bf16[3,512,128]{1,2,0:T(8,128)(2,1)}, bf16[3,512,128]{1,2,0:T(8,128)(2,1)}) async-done(((bf16[3,512,128]{1,2,0:T(8,128)(2,1)}, bf16[3,512,128]{1,2,0:T(8,128)(2,1)}), (bf16[3,512,128]{1,2,0:T(8,128)(2,1)}, bf16[3,512,128]{1,2,0:T(8,128)(2,1)})) %all-reduce.13.cloned.1.call-update) | async-done | bytes 786448 | tf_op jit(solution)/shard_map/psum | solution.py:14
  320.5 1.2 copy.225
  321.7 73.2 %all-reduce.9.cloned.1.call-done = (bf16[2,512,128]{1,2,0:T(8,128)(2,1)}, bf16[2,512,128]{1,2,0:T(8,128)(2,1)}) async-done(((bf16[2,512,128]{1,2,0:T(8,128)(2,1)}, bf16[2,512,128]{1,2,0:T(8,128)(2,1)}), (bf16[2,512,128]{1,2,0:T(8,128)(2,1)}, bf16[2,512,128]{1,2,0:T(8,128)(2,1)})) %all-reduce.9.cloned.1.call-update) | async-done | bytes 524304 | tf_op jit(solution)/shard_map/psum | solution.py:14
  394.9 1.0 broadcast_in_dim.178
  398.0 1.6 convolution_multiply_fusion
  399.6 2.6 fusion.137
  402.5 1.0 fusion.69
  403.4 71.4 %custom-call.22 = f32[3,2,128,128]{3,2,1,0:T(8,128)S(1)} custom-call(f32[3,2,128,128]{3,2,1,0:T(8,128)} %fusion.69), custom_call_target="Cholesky" | custom-call | tf_op jit(solution)/shard_map/jit(cholesky)/cholesky | solution.py:36
  475.2 59.0 %custom-call.23 = f32[3,2,1,128,128]{3,4,2,1,0:T(8,128)S(1)} custom-call(f32[3,2,1,128,128]{4,3,2,1,0:T(8,128)S(1)} %select_bitcast_fusion), custom_call_target="InvertDiagBlocksLowerTriangular" | custom-call | tf_op jit(solution)/shard_map/triangular_solve | solution.py:37
  534.1 1.5 fusion.66
  535.7 1.4 fusion.41
  537.6 1.2 copy.238
  539.2 1.1 fusion.5
  540.3 1.2 copy.239
  (199 shorter events, 15.2 us)
Async XLA Ops:
  7.2 127.6 %copy-start = (bf16[512,128]{1,0:T(8,128)(2,1)S(1)}, bf16[512,128]{1,0:T(8,128)(2,1)}, u32[]{:S(2)}) copy-start(bf16[512,128]{1,0:T(8,128)(2,1)} %param.38) | copy-start | bytes 393220
  7.2 1.6 copy-start.55
  7.2 2.3 copy-start.16
  7.2 48.5 %all-reduce.15.cloned.1.call-start = ((), (), s32[]{:S(2)}) async-start(), calls=%async_computation.3 | async-start | bytes 1572864 | tf_op jit(solution)/shard_map/psum | solution.py:14
  8.8 1.1 copy-start.44
  15.3 3.1 copy-start.59
  19.5 1.9 copy-start.11
  19.6 110.7 %all-reduce.11.cloned.1.call-start = ((), (), s32[]{:S(2)}) async-start(), calls=%async_computation.1 | async-start | bytes 1048576 | tf_op jit(solution)/shard_map/psum | solution.py:14
  19.7 1.7 copy-start.1
  20.5 1.7 copy-start.42
  20.5 3.0 copy-start.45
  20.5 300.0 %all-reduce.13.cloned.1.call-start = ((), (), s32[]{:S(2)}) async-start(), calls=%async_computation.2 | async-start | bytes 1572864 | tf_op jit(solution)/shard_map/psum | solution.py:14
  21.4 112.2 %copy-start.19 = (f32[128,128]{1,0:T(8,128)}, f32[128,128]{1,0:T(8,128)S(1)}, u32[]{:S(2)}) copy-start(f32[128,128]{1,0:T(8,128)S(1)} %fusion.116) | copy-start | bytes 196612
  21.4 139.5 %copy-start.22 = (pred[128,128]{1,0:T(8,128)(4,1)}, pred[128,128]{1,0:T(8,128)(4,1)S(1)}, u32[]{:S(2)}) copy-start(pred[128,128]{1,0:T(8,128)(4,1)S(1)} %iota_compare_fusion.1) | copy-start | bytes 49156
  22.8 111.0 %copy-start.61 = (pred[3]{0:T(512)(128)(4,1)}, pred[3]{0:T(512)(128)(4,1)S(1)}, u32[]{:S(2)}) copy-start(pred[3]{0:T(512)(128)(4,1)S(1)} %broadcast_compare_fusion.3) | copy-start | bytes 13
  24.7 109.1 %copy-start.56 = (pred[2]{0:T(512)(128)(4,1)}, pred[2]{0:T(512)(128)(4,1)S(1)}, u32[]{:S(2)}) copy-start(pred[2]{0:T(512)(128)(4,1)S(1)} %get-tuple-element.176) | copy-start | bytes 10
  24.8 157.7 %copy-start.14 = (f32[128,128]{0,1:T(8,128)}, f32[128,128]{0,1:T(8,128)S(1)}, u32[]{:S(2)}) copy-start(f32[128,128]{0,1:T(8,128)S(1)} %copy.190) | copy-start | bytes 196612
  55.7 77.9 %copy-start.13 = (bf16[3,512,128]{1,2,0:T(8,128)(2,1)S(1)}, bf16[3,512,128]{1,2,0:T(8,128)(2,1)}, u32[]{:S(2)}) copy-start(bf16[3,512,128]{1,2,0:T(8,128)(2,1)} %get-tuple-element.139) | copy-start | bytes 1179652
  130.2 3.8 copy-start.32
  130.2 4.5 copy-start.35
  182.4 1.4 copy-start.28
  240.2 2.4 copy-start.40
  240.2 2.4 copy-start.51
  242.6 1.7 copy-start.46
  242.6 3.8 copy-start.54
  244.1 4.1 copy-start.57
  248.2 3.1 copy-start.10
  250.3 1.6 copy-start.2
  250.3 1.6 copy-start.33
  250.3 1.6 copy-start.36
  250.3 1.6 copy-start.53
  251.2 1.1 copy-start.5
  251.2 1.2 copy-start.6
  251.2 1.3 copy-start.9
  251.9 1.2 copy-start.12
  251.9 1.2 copy-start.29
  251.9 1.2 copy-start.34
  252.0 1.2 copy-start.52
  253.2 1.2 copy-start.60
  253.2 1.2 copy-start.62
  254.4 1.2 copy-start.21
  255.6 0.8 copy-start.49
  255.6 1.5 copy-start.15
  255.6 1.6 copy-start.48
  256.4 26.8 %copy-start.23 = (pred[128,128]{1,0:T(8,128)(4,1)S(1)}, pred[128,128]{1,0:T(8,128)(4,1)}, u32[]{:S(2)}) copy-start(pred[128,128]{1,0:T(8,128)(4,1)} %copy-done.22) | copy-start | bytes 49156
  256.5 26.9 %copy-start.26 = (bf16[3,512,128]{1,2,0:T(8,128)(2,1)S(1)}, bf16[3,512,128]{1,2,0:T(8,128)(2,1)}, u32[]{:S(2)}) copy-start(bf16[3,512,128]{1,2,0:T(8,128)(2,1)} %get-tuple-element.170) | copy-start | bytes 1179652
  284.2 110.7 %all-reduce.9.cloned.1.call-start = ((), (), s32[]{:S(2)}) async-start(), calls=%async_computation | async-start | bytes 1048576 | tf_op jit(solution)/shard_map/psum | solution.py:14
  305.0 2.1 copy-start.31
  305.0 2.1 copy-start.38
  305.0 2.1 copy-start.50
  307.5 89.1 %copy-start.7 = (bf16[3,2,512,128]{2,3,1,0:T(8,128)(2,1)}, bf16[3,2,512,128]{2,3,1,0:T(8,128)(2,1)S(1)}, u32[]{:S(2)}) copy-start(bf16[3,2,512,128]{2,3,1,0:T(8,128)(2,1)S(1)} %fusion.40) | copy-start | bytes 2359300
  395.9 0.9 copy-start.17
  395.9 1.3 copy-start.25
  395.9 1.3 copy-start.39
  396.9 1.1 copy-start.43
  398.0 1.6 copy-start.3
  399.6 2.9 copy-start.20
  399.6 2.9 copy-start.27
  399.6 2.9 copy-start.41
  402.3 72.5 %copy-start.24 = (pred[128,128]{1,0:T(8,128)(4,1)S(1)}, pred[128,128]{1,0:T(8,128)(4,1)}, u32[]{:S(2)}) copy-start(pred[128,128]{1,0:T(8,128)(4,1)} %copy-done.22) | copy-start | bytes 49156
  534.1 1.5 copy-start.4
  535.7 1.4 copy-start.58
  537.6 1.2 copy-start.8
  537.6 1.6 copy-start.18
  (3 other events, 2.2 us)
Sparse Core Ops, SparseCore 0:
  19.7 35.9 all-reduce.14
  59.2 71.0 all-reduce.10
  284.3 36.1 all-reduce.12
  323.8 71.0 all-reduce.8
where the time goes:
time: 558 us; the launch traced here: 548 us
  other arithmetic  285 us (51%)
  waiting for transfers between devices  186 us (33%)
  matrix products  37.8 us (7%)
  local copies, waits for them, and re-layouts  22.4 us (4%)
  between operations  16.6 us (3%)
    psum x4, waiting for transfers between devices, from_root(): return lax.psum(jnp.where(mine, array, jnp.zeros_like(array)), axis)  186 us
    another operation x13, other arithmetic, compress(): factor = jnp.linalg.cholesky(gram_matrix)  146 us
    another operation x9, other arithmetic, compress(): lax.linalg.triangular_solve(factor, jnp.swapaxes(sample, -1, -2), left_si...  122 us
  transfers between devices with their start and end apart: 4, of which 4 were waited for; matrix products, arithmetic and copies ran while one was open for 6% of the time, Pallas kernels for 0%

commit v1 on v0

v1 whole, which is shorter than its diff:
```python
import functools

import jax
import jax.numpy as jnp
from jax import lax
from jax.experimental import pallas as pl
from jax.experimental.pallas import tpu as pltpu
from jax.sharding import PartitionSpec as P

PANELS = 2
GROUP = 8
BLOCK = 32
F32 = jnp.float32
BF16 = jnp.bfloat16

NN = (((1,), (0,)), ((), ()))
NT = (((1,), (1,)), ((), ()))
TN = (((0,), (0,)), ((), ()))


def mm(left, right, dims=NN):
    return lax.dot_general(left, right, dims, preferred_element_type=F32)


def halves(value):
    high = value.astype(BF16)
    low = (value - high.astype(F32)).astype(BF16)
    return high, low


def inverse_factor(gram):
    tiles, size, _ = gram.shape
    lane = lax.broadcasted_iota(jnp.int32, (1, 1, size), 2)
    sub = lax.broadcasted_iota(jnp.int32, (1, GROUP, 1), 1)
    below = gram
    done = []
    for first in range(0, size, BLOCK):
        groups = [
            below[:, at : at + GROUP, :] for at in range(0, BLOCK, GROUP)
        ]
        scales = []
        for step in range(BLOCK):
            pivot = first + step
            home, line = divmod(step, GROUP)
            own = groups[home]
            row = own[:, line : line + 1, :]
            inverse = 1.0 / row[:, :, pivot : pivot + 1]
            at_pivot = lane == pivot
            turned = jnp.where(at_pivot, 1.0, row) * inverse
            for g in range(home, BLOCK // GROUP):
                value = groups[g]
                column = value[:, :, pivot : pivot + 1]
                fresh = jnp.where(at_pivot, 0.0, value) - column * turned
                groups[g] = jnp.where(sub > line, fresh, value) if g == home else fresh
        block = jnp.concatenate(groups, axis=1)
        row_id = first + lax.broadcasted_iota(jnp.int32, (1, BLOCK, 1), 1)
        diagonal = jnp.sum(jnp.where(lane == row_id, block, 0.0), axis=2, keepdims=True)
        block = jnp.where(lane == row_id, 1.0, block) * lax.rsqrt(diagonal)
        inner = (lane >= first) & (lane < first + BLOCK)
        block = jnp.where(inner & (lane > row_id), 0.0, block)
        done.append(jnp.where(lane > row_id, 0.0, block))
        if first + BLOCK < size:
            rest = below[:, BLOCK:, :]
            parts = []
            for t in range(tiles):
                spread = block[t].T[first + BLOCK :, :]
                parts.append(
                    jnp.where(inner[0], 0.0, rest[t])
                    - lax.dot_general(
                        spread,
                        block[t],
                        NN,
                        precision=lax.Precision.HIGHEST,
                        preferred_element_type=F32,
                    )
                )
            below = jnp.stack(parts)
    return jnp.concatenate(done, axis=1)


def panel_kernel(
    panel,
    row_size,
    col_size,
    ranks_ref,
    u_ref,
    v_ref,
    top_u_ref,
    top_v_ref,
    left_u_ref,
    left_v_ref,
    lower_ref,
    upper_ref,
    order_ref,
    sketch_ref,
    out_u_ref,
    out_v_ref,
    turned_ref,
    side_ref,
    x_ref,
    s_ref,
):
    row_tiles, col_tiles, tile_size, rank_width = u_ref.shape
    rows = [lax.axis_index("row") + a * row_size for a in range(row_tiles)]
    cols = [lax.axis_index("col") + e * col_size for e in range(col_tiles)]
    tiles = [(a, e) for a in range(row_tiles) for e in range(col_tiles)]

    place = lax.broadcasted_iota(jnp.int32, (tile_size, tile_size), 1)
    chosen = jnp.where(order_ref[...] == place, 1.0, 0.0).astype(BF16)
    for e in range(col_tiles):
        raw = top_u_ref[e]
        permuted = mm(chosen, raw).astype(BF16)
        turned = mm(lower_ref[...], permuted).astype(BF16)
        turned_ref[e] = jnp.where(cols[e] > panel, turned, raw)
    for a in range(row_tiles):
        raw = left_v_ref[a]
        turned = (mm(upper_ref[...], raw, TN) * tile_size**0.5).astype(BF16)
        side_ref[a] = jnp.where(rows[a] > panel, turned, raw)

    sketch = sketch_ref[...]
    top_probe = [mm(sketch, top_v_ref[e], TN) for e in range(col_tiles)]
    row_at = lax.broadcasted_iota(jnp.int32, (rank_width, 1), 0)
    diag = row_at == lax.broadcasted_iota(jnp.int32, (rank_width, rank_width), 1)
    grams = []
    for t, (a, e) in enumerate(tiles):
        coupling = (mm(side_ref[a], turned_ref[e], TN) * tile_size**-0.5).astype(BF16)
        update = (mm(left_u_ref[a], coupling) * rank_width**-0.5).astype(BF16)
        x = jnp.concatenate([u_ref[a, e], -update], axis=1)
        x_ref[t] = x
        probe = jnp.concatenate([mm(sketch, v_ref[a, e], TN), top_probe[e]], axis=1)
        keep = row_at < ranks_ref[t]
        probe = jnp.where(keep, probe, 0.0)
        high, low = halves(probe)
        sample = mm(high, x, NT) + mm(low, x, NT)
        s_ref[t] = sample
        high, low = halves(sample)
        cross = mm(high, low, NT)
        gram = mm(high, high, NT) + (cross + cross.T)
        grams.append(gram + jnp.where(diag & ~keep, 1.0, 0.0))
    inverse = inverse_factor(jnp.stack(grams))
    for t, (a, e) in enumerate(tiles):
        high, low = halves(inverse[t])
        s_high, s_low = halves(s_ref[t])
        basis = mm(high, s_high) + (mm(high, s_low) + mm(low, s_high))
        fresh_u = (basis * tile_size**0.5).T.astype(BF16)
        x = x_ref[t]
        high, low = halves(basis)
        weights = mm(high, x) + mm(low, x)
        w_high, w_low = halves(weights)
        y = jnp.concatenate([v_ref[a, e], top_v_ref[e]], axis=1)
        fresh_v = ((mm(y, w_high, NT) + mm(y, w_low, NT)) * tile_size**-0.5).astype(BF16)
        old_u, old_v = u_ref[a, e], v_ref[a, e]
        if a == 0:
            old_u = jnp.where(rows[a] == panel, turned_ref[e], old_u)
        if e == 0:
            old_v = jnp.where(cols[e] == panel, side_ref[a], old_v)
        active = (rows[a] > panel) & (cols[e] > panel)
        out_u_ref[a, e] = jnp.where(active, fresh_u, old_u)
        out_v_ref[a, e] = jnp.where(active, fresh_v, old_v)


def from_root(array, axis, root):
    mine = lax.axis_index(axis) == root
    return lax.psum(jnp.where(mine, array, jnp.zeros_like(array)), axis)


def on_device(
    row_size, col_size, tile_u, tile_v, tile_ranks, lower_inverse, upper_inverse, row_order, sketch
):
    row_tiles, col_tiles = tile_u.shape[0], tile_u.shape[2]
    tile_size, rank_width = tile_u.shape[4], tile_u.shape[5]
    shape_four = (row_tiles, col_tiles, tile_size, rank_width)
    ranks = tile_ranks.reshape(row_tiles, col_tiles)
    keep = (jnp.arange(rank_width, dtype=jnp.int32) < ranks[:, :, None]).astype(BF16)
    u = tile_u.reshape(shape_four) * keep[:, :, None, :]
    v = tile_v.reshape(shape_four) * keep[:, :, None, :]
    ranks = ranks.reshape(-1)
    tiles = row_tiles * col_tiles
    vmem = pl.BlockSpec(memory_space=pltpu.VMEM)
    for panel in range(PANELS):
        top = from_root(jnp.stack([u[0], v[0]]), "row", panel)
        left = from_root(jnp.stack([u[:, 0], v[:, 0]]), "col", panel)
        u, v = pl.pallas_call(
            functools.partial(panel_kernel, panel, row_size, col_size),
            out_shape=(
                jax.ShapeDtypeStruct(shape_four, BF16),
                jax.ShapeDtypeStruct(shape_four, BF16),
            ),
            in_specs=[pl.BlockSpec(memory_space=pltpu.SMEM)] + [vmem] * 10,
            out_specs=(vmem, vmem),
            scratch_shapes=[
                pltpu.VMEM((col_tiles, tile_size, rank_width), BF16),
                pltpu.VMEM((row_tiles, tile_size, rank_width), BF16),
                pltpu.VMEM((tiles, tile_size, 2 * rank_width), BF16),
                pltpu.VMEM((tiles, rank_width, tile_size), F32),
            ],
            name=f"panel_{panel}",
        )(
            ranks,
            u,
            v,
            top[0],
            top[1],
            left[0],
            left[1],
            lower_inverse[panel],
            upper_inverse[panel],
            row_order[panel].reshape(tile_size, 1),
            sketch,
        )
    return u.reshape(tile_u.shape), v.reshape(tile_v.shape)


def solution(mesh):
    tile_spec = P(None, "row", None, "col", None, None)
    return jax.shard_map(
        functools.partial(on_device, mesh.shape["row"], mesh.shape["col"]),
        mesh=mesh,
        in_specs=(tile_spec, tile_spec, P(None, "row", None, "col"), P(), P(), P(), P()),
        out_specs=(tile_spec, tile_spec),
        check_vma=False,
    )
```

time: 558 us -> 300 us (0.54); the launches traced: 548 us -> 296 us
  other arithmetic: 285 us -> 5.24 us
  Pallas kernels: 0 us -> 51.7 us
  matrix products: 37.8 us -> 0 us
  waiting for transfers between devices: 186 us -> 206 us
    another operation x22 -> x0, other arithmetic: 268 us -> none  [the longest x13 146 us: compress(): factor = jnp.linalg.cholesky(gram_matrix)]
    pallas_call x0 -> x2, Pallas kernels: none -> 51.7 us  [on_device(): pl.pallas_call(functools.partial(panel_kernel, panel, row_size, col_size)...]
    dot_general x30 -> x0, matrix products: 31.1 us -> none  [the longest x4 7.14 us: compress(): jnp.einsum('...br,...bs->...rs', sample, sample, precision=HIGHEST)]
    psum x4, waiting for transfers between devices: 186 us -> 206 us  [from_root(): return lax.psum(jnp.where(mine, array, jnp.zeros_like(array)), axis)]
    squeeze x4 -> x5, local copies, waits for them, and re-layouts: 0.36 us -> 9.21 us  [the longest x2 4.11 us: on_device(): left[1]]
    another operation x4 -> x0, matrix products: 6.76 us -> none  [compress(): lax.linalg.triangular_solve(factor, jnp.swapaxes(sample, -1, -2), left_si...]
  transfers between devices with their start and end apart: 4 -> 4, of which waited for: 4 -> 4; matrix products, arithmetic and copies ran while one was open for 6% -> 4% of each run, Pallas kernels for 0% -> 0%
where the time goes in v1:
time: 300 us; the launch traced here: 296 us
  waiting for transfers between devices  206 us (69%)
  Pallas kernels  51.7 us (17%)
  local copies, waits for them, and re-layouts  18.6 us (6%)
  between operations  13.9 us (5%)
  other arithmetic  5.24 us (2%)
    psum x4, waiting for transfers between devices, from_root(): return lax.psum(jnp.where(mine, array, jnp.zeros_like(array)), axis)  206 us
    pallas_call x2, Pallas kernels, on_device(): pl.pallas_call(functools.partial(panel_kernel, panel, row_size, col_size)...  51.7 us
  transfers between devices with their start and end apart: 4, of which 4 were waited for; matrix products, arithmetic and copies ran while one was open for 4% of the time, Pallas kernels for 0%

profile of v1, /device:TPU:28, one launch (start us, length us, event | category | flops | bytes accessed | tf_op | source)
XLA Modules:
  0.0 296.2 jit_solution(14181762960697436272)
XLA Ops:
  7.2 0.0 all-reduce.7.cloned.1.call-start
  7.2 0.0 copy-start.5
  7.2 0.7 copy-done.5
  7.9 0.1 fusion
  8.0 1.5 bitcast_multiply_fusion
  9.4 0.1 slice_bitcast_fusion.10
  9.5 1.0 maximum_select_fusion
  10.5 0.0 all-reduce.7.cloned.1.call-update
  10.5 0.0 all-reduce.5.cloned.1.call-start
  10.6 0.9 maximum_select_fusion.2
  11.5 0.0 all-reduce.5.cloned.1.call-update
  11.5 0.0 all-reduce.11.cloned.1.call-start
  11.6 0.0 copy-start.4
  11.6 0.9 copy.23.u_ref
  12.5 0.0 copy-start.6
  12.5 0.0 copy-start.3
  12.5 0.9 copy.24.v_ref
  13.5 0.1 copy.20
  13.6 0.0 copy-done.6
  13.6 0.9 copy.25.order_ref
  14.5 0.7 reshape_reshape.3.ranks_ref
  15.1 0.0 copy-done.4
  15.1 0.0 copy-done.3
  15.1 1.4 slice_bitcast_fusion
  16.5 30.1 %all-reduce.7.cloned.1.call-done = bf16[2,3,512,128]{3,2,1,0:T(8,128)(2,1)} async-done(((bf16[2,3,512,128]{3,2,1,0:T(8,128)(2,1)}), bf16[2,3,512,128]{3,2,1,0:T(8,128)(2,1)}) %all-reduce.7.cloned.1.call-update) | async-done | bytes 786448 | tf_op jit(solution)/shard_map/psum | solution.py:164
  46.6 2.1 slice_bitcast_fusion.8
  48.7 72.3 %all-reduce.5.cloned.1.call-done = bf16[2,2,512,128]{3,2,0,1:T(8,128)(2,1)} async-done(((bf16[2,2,512,128]{3,2,0,1:T(8,128)(2,1)}), bf16[2,2,512,128]{3,2,0,1:T(8,128)(2,1)}) %all-reduce.5.cloned.1.call-update) | async-done | bytes 524304 | tf_op jit(solution)/shard_map/psum | solution.py:164
  121.0 1.9 slice_bitcast_fusion.14
  122.9 25.9 %panel_0.1 = (bf16[3,2,512,128]{3,2,1,0:T(8,128)(2,1)}, bf16[3,2,512,128]{3,2,1,0:T(8,128)(2,1)}) custom-call(s32[6]{0:T(128)} %reshape_reshape.3.ranks_ref, bf16[3,2,512,128]{3,2,1,0:T(8,128)(2,1)} %copy.23.u_ref, bf16[3,2,512,128]{3,2,1,0:T(8,128)(2,1)} %copy.24.v_ref, bf16[2,512,128]{2,1,0:T(8,128)(2,1)} %get-tuple-element.25.top_u_ref, ...), custom_call_target="tpu_custom_call" | custom-call | tf_op jit(solution)/shard_map/panel_0/pallas_call | solution.py:183
  148.8 0.0 copy-start
  148.8 1.1 slice_bitcast_fusion.6
  149.9 0.2 copy-done
  150.1 1.0 maximum_select_fusion.1
  151.0 0.0 all-reduce.11.cloned.1.call-update
  151.1 0.2 all-reduce.9.cloned.1.call-start
  151.3 0.0 copy-start.1
  151.3 0.1 copy.26
  151.4 1.1 copy-done.1
  152.4 0.0 copy-start.2
  152.4 0.1 copy.27
  152.5 0.8 copy-done.2
  153.3 0.0 slice-start
  153.3 0.9 slice-done
  154.3 0.9 maximum_select_fusion.3
  155.1 0.0 all-reduce.9.cloned.1.call-update
  155.1 0.9 copy.30.order_ref
  156.0 31.2 %all-reduce.11.cloned.1.call-done = bf16[2,3,512,128]{3,2,1,0:T(8,128)(2,1)} async-done(((bf16[2,3,512,128]{3,2,1,0:T(8,128)(2,1)}), bf16[2,3,512,128]{3,2,1,0:T(8,128)(2,1)}) %all-reduce.11.cloned.1.call-update) | async-done | bytes 786448 | tf_op jit(solution)/shard_map/psum | solution.py:164
  187.2 2.0 slice_bitcast_fusion.4
  189.2 72.8 %all-reduce.9.cloned.1.call-done = bf16[2,2,512,128]{3,2,0,1:T(8,128)(2,1)} async-done(((bf16[2,2,512,128]{3,2,0,1:T(8,128)(2,1)}), bf16[2,2,512,128]{3,2,0,1:T(8,128)(2,1)}) %all-reduce.9.cloned.1.call-update) | async-done | bytes 524304 | tf_op jit(solution)/shard_map/psum | solution.py:164
  262.0 1.9 slice_bitcast_fusion.12
  263.8 25.9 %panel_1.1 = (bf16[3,2,512,128]{3,2,1,0:T(8,128)(2,1)}, bf16[3,2,512,128]{3,2,1,0:T(8,128)(2,1)}) custom-call(s32[6]{0:T(128)} %reshape_reshape.3.ranks_ref, bf16[3,2,512,128]{3,2,1,0:T(8,128)(2,1)} %get-tuple-element.6.u_ref, bf16[3,2,512,128]{3,2,1,0:T(8,128)(2,1)} %get-tuple-element.7.v_ref, bf16[2,512,128]{2,1,0:T(8,128)(2,1)} %get-tuple-element.23.top_u_ref, ...), custom_call_target="tpu_custom_call" | custom-call | tf_op jit(solution)/shard_map/panel_1/pallas_call | solution.py:183
  (5 shorter events, 0.1 us)
Async XLA Ops:
  7.2 39.5 %all-reduce.7.cloned.1.call-start = ((), (), s32[]{:S(2)}) async-start(), calls=%async_computation.1 | async-start | bytes 1572864 | tf_op jit(solution)/shard_map/psum | solution.py:164
  7.2 0.7 copy-start.5
  10.5 110.5 %all-reduce.5.cloned.1.call-start = ((), (), s32[]{:S(2)}) async-start(), calls=%async_computation | async-start | bytes 1048576 | tf_op jit(solution)/shard_map/psum | solution.py:164
  11.5 175.6 %all-reduce.11.cloned.1.call-start = ((), (), s32[]{:S(2)}) async-start(), calls=%async_computation.3 | async-start | bytes 1572864 | tf_op jit(solution)/shard_map/psum | solution.py:164
  11.6 3.5 %copy-start.4 = (bf16[2,512,512]{2,1,0:T(8,128)(2,1)S(1)}, bf16[2,512,512]{2,1,0:T(8,128)(2,1)}, u32[]{:S(2)}) copy-start(bf16[2,512,512]{2,1,0:T(8,128)(2,1)} %param.10) | copy-start | bytes 3145732
  12.5 1.0 copy-start.6
  12.5 2.6 copy-start.3
  148.8 1.3 copy-start
  151.1 110.9 %all-reduce.9.cloned.1.call-start = ((), (), s32[]{:S(2)}) async-start(), calls=%async_computation.2 | async-start | bytes 1048576 | tf_op jit(solution)/shard_map/psum | solution.py:164
  151.3 1.1 copy-start.1
  152.4 0.9 copy-start.2
  153.3 0.9 slice-start
Sparse Core Ops, SparseCore 0:
  10.6 35.9 all-reduce.6
  50.0 70.9 all-reduce.4
  151.2 35.9 all-reduce.10
  191.0 70.9 all-reduce.8

commit v2 on v1

v2 whole, which is shorter than its diff:
```python
import functools

import jax
import jax.numpy as jnp
from jax import lax
from jax.experimental import pallas as pl
from jax.experimental.pallas import tpu as pltpu
from jax.sharding import PartitionSpec as P

PANELS = 2
GROUP = 8
BLOCK = 32
CHUNKS = 4
F32 = jnp.float32
BF16 = jnp.bfloat16

NN = (((1,), (0,)), ((), ()))
NT = (((1,), (1,)), ((), ()))
TN = (((0,), (0,)), ((), ()))


def mm(left, right, dims=NN):
    return lax.dot_general(left, right, dims, preferred_element_type=F32)


def halves(value):
    high = value.astype(BF16)
    low = (value - high.astype(F32)).astype(BF16)
    return high, low


def inverse_factor(gram):
    tiles, size, _ = gram.shape
    lane = lax.broadcasted_iota(jnp.int32, (1, 1, size), 2)
    sub = lax.broadcasted_iota(jnp.int32, (1, GROUP, 1), 1)
    below = gram
    done = []
    for first in range(0, size, BLOCK):
        groups = [
            below[:, at : at + GROUP, :] for at in range(0, BLOCK, GROUP)
        ]
        scales = []
        for step in range(BLOCK):
            pivot = first + step
            home, line = divmod(step, GROUP)
            own = groups[home]
            row = own[:, line : line + 1, :]
            inverse = 1.0 / row[:, :, pivot : pivot + 1]
            at_pivot = lane == pivot
            turned = jnp.where(at_pivot, 1.0, row) * inverse
            for g in range(home, BLOCK // GROUP):
                value = groups[g]
                column = value[:, :, pivot : pivot + 1]
                fresh = jnp.where(at_pivot, 0.0, value) - column * turned
                groups[g] = jnp.where(sub > line, fresh, value) if g == home else fresh
        block = jnp.concatenate(groups, axis=1)
        row_id = first + lax.broadcasted_iota(jnp.int32, (1, BLOCK, 1), 1)
        diagonal = jnp.sum(jnp.where(lane == row_id, block, 0.0), axis=2, keepdims=True)
        block = jnp.where(lane == row_id, 1.0, block) * lax.rsqrt(diagonal)
        inner = (lane >= first) & (lane < first + BLOCK)
        block = jnp.where(inner & (lane > row_id), 0.0, block)
        done.append(jnp.where(lane > row_id, 0.0, block))
        if first + BLOCK < size:
            rest = below[:, BLOCK:, :]
            parts = []
            for t in range(tiles):
                spread = block[t].T[first + BLOCK :, :]
                parts.append(
                    jnp.where(inner[0], 0.0, rest[t])
                    - lax.dot_general(
                        spread,
                        block[t],
                        NN,
                        precision=lax.Precision.HIGHEST,
                        preferred_element_type=F32,
                    )
                )
            below = jnp.stack(parts)
    return jnp.concatenate(done, axis=1)


class Tree:
    def __init__(self, axis, size, root):
        place = lax.axis_index(axis)
        self.axis = axis
        self.pair = place + 1 - 2 * lax.rem(place, 2)
        self.chain = lax.rem(place, 2) == root
        self.is_root = place == root
        self.has_next = self.chain & (place + 2 < size)
        self.next = jnp.minimum(place + 2, size - 1)
        self.parent = jnp.where(self.chain, jnp.maximum(place - 2, 0), self.pair)
        self.place = place

    def greet(self, barrier):
        @pl.when(~self.is_root)
        def _():
            self.signal(barrier, self.parent)

        @pl.when(self.chain)
        def _():
            self.signal(barrier, self.pair)

        @pl.when(self.has_next)
        def _():
            self.signal(barrier, self.next)

    def signal(self, barrier, place):
        pl.semaphore_signal(
            barrier, inc=1, device_id={self.axis: place}, device_id_type=pl.DeviceIdType.MESH
        )

    def met(self):
        return (
            (~self.is_root).astype(jnp.int32)
            + self.chain.astype(jnp.int32)
            + self.has_next.astype(jnp.int32)
        )

    def copy(self, source, target, send_sem, recv_sem, place):
        return pltpu.make_async_remote_copy(
            src_ref=source,
            dst_ref=target,
            send_sem=send_sem,
            recv_sem=recv_sem,
            device_id={self.axis: place},
            device_id_type=pl.DeviceIdType.MESH,
        )

    def send(self, source, target, sends, recv, c):
        @pl.when(self.has_next)
        def _():
            self.copy(source, target, sends.at[c, 0], recv.at[c], self.next).start()

        @pl.when(self.chain)
        def _():
            self.copy(source, target, sends.at[c, 1], recv.at[c], self.pair).start()

    def sent(self, target, sends, recv, c):
        @pl.when(self.has_next)
        def _():
            self.copy(target, target, sends.at[c, 0], recv.at[c], self.next).wait_send()

        @pl.when(self.chain)
        def _():
            self.copy(target, target, sends.at[c, 1], recv.at[c], self.pair).wait_send()

    def received(self, target, sends, recv, c):
        self.copy(target, target, sends.at[c, 0], recv.at[c], self.parent).wait_recv()


def panels_kernel(
    row_size,
    col_size,
    ranks_ref,
    u_ref,
    v_ref,
    lower_ref,
    upper_ref,
    order_ref,
    sketch_ref,
    out_u_ref,
    out_v_ref,
    top_ref,
    left_ref,
    moved_ref,
    turned_ref,
    side_ref,
    x_ref,
    s_ref,
    top_send,
    top_recv,
    left_send,
    left_recv,
):
    row_tiles, col_tiles, tile_size, rank_width = u_ref.shape
    rows = [lax.axis_index("row") + a * row_size for a in range(row_tiles)]
    cols = [lax.axis_index("col") + e * col_size for e in range(col_tiles)]
    tiles = [(a, e) for a in range(row_tiles) for e in range(col_tiles)]
    early = [t for t, (a, e) in enumerate(tiles) if a == 0 or e == 0]
    late = [t for t, (a, e) in enumerate(tiles) if a > 0 and e > 0]
    piece = tile_size // CHUNKS
    row_trees = [Tree("row", row_size, panel) for panel in range(PANELS)]
    col_trees = [Tree("col", col_size, panel) for panel in range(PANELS)]

    barrier = pltpu.get_barrier_semaphore()
    met = 0
    for tree in row_trees + col_trees:
        tree.greet(barrier)
        met = met + tree.met()
    pl.semaphore_wait(barrier, met)

    def flows(panel):
        u_from, v_from = (u_ref, v_ref) if panel == 0 else (out_u_ref, out_v_ref)
        top, left = [], []
        for which, ref in ((1, v_from), (0, u_from)):
            for q in range(CHUNKS):
                part = pl.ds(q * piece, piece)
                for e in range(col_tiles):
                    top.append((ref.at[0, e, part], top_ref.at[panel, which, e, part]))
                for a in range(row_tiles):
                    left.append((ref.at[a, 0, part], left_ref.at[panel, which, a, part]))
        return [
            (row_trees[panel], top, top_send.at[panel], top_recv.at[panel]),
            (col_trees[panel], left, left_send.at[panel], left_recv.at[panel]),
        ]

    def launch(panel):
        u_from, v_from = (u_ref, v_ref) if panel == 0 else (out_u_ref, out_v_ref)
        for tree, pieces, sends, recv in flows(panel):

            @pl.when(tree.is_root)
            def _():
                for c, (source, target) in enumerate(pieces):
                    tree.send(source, target, sends, recv, c)

        @pl.when(row_trees[panel].is_root)
        def _():
            top_ref[panel, 0] = u_from[0]
            top_ref[panel, 1] = v_from[0]

        @pl.when(col_trees[panel].is_root)
        def _():
            left_ref[panel, 0] = u_from[:, 0]
            left_ref[panel, 1] = v_from[:, 0]

    def relay(panel):
        pending = [
            (c / len(pieces), which, c)
            for which, (_, pieces, _, _) in enumerate(flows(panel))
            for c in range(len(pieces))
        ]
        for _, which, c in sorted(pending):
            tree, pieces, sends, recv = flows(panel)[which]
            target = pieces[c][1]

            @pl.when(~tree.is_root)
            def _():
                tree.received(target, sends, recv, c)
                tree.send(target, target, sends, recv, c)

    def settle(panel):
        for tree, pieces, sends, recv in flows(panel):
            for c, (_, target) in enumerate(pieces):
                tree.sent(target, sends, recv, c)

    launch(0)
    place = lax.broadcasted_iota(jnp.int32, (tile_size, tile_size), 0)
    for panel in range(PANELS):
        chosen = jnp.where(order_ref[panel : panel + 1, :] == place, 1.0, 0.0).astype(BF16)
        moved_ref[panel] = mm(lower_ref[panel], chosen, NT).astype(BF16)

    row_at = lax.broadcasted_iota(jnp.int32, (rank_width, 1), 0)
    diag = row_at == lax.broadcasted_iota(jnp.int32, (rank_width, rank_width), 1)
    sketch = sketch_ref[...]
    for panel in range(PANELS):
        from_u, from_v = (u_ref, v_ref) if panel == 0 else (out_u_ref, out_v_ref)
        relay(panel)
        for e in range(col_tiles):
            raw = top_ref[panel, 0, e]
            turned = mm(moved_ref[panel], raw).astype(BF16)
            turned_ref[e] = jnp.where(cols[e] > panel, turned, raw)
        for a in range(row_tiles):
            raw = left_ref[panel, 1, a]
            turned = (mm(upper_ref[panel], raw, TN) * tile_size**0.5).astype(BF16)
            side_ref[a] = jnp.where(rows[a] > panel, turned, raw)

        top_probe = [mm(sketch, top_ref[panel, 1, e], TN) for e in range(col_tiles)]
        grams = []
        for t, (a, e) in enumerate(tiles):
            coupling = (mm(side_ref[a], turned_ref[e], TN) * tile_size**-0.5).astype(BF16)
            update = (mm(left_ref[panel, 0, a], coupling) * rank_width**-0.5).astype(BF16)
            x = jnp.concatenate([from_u[a, e], -update], axis=1)
            x_ref[t] = x
            probe = jnp.concatenate([mm(sketch, from_v[a, e], TN), top_probe[e]], axis=1)
            keep = row_at < ranks_ref[t]
            probe = jnp.where(keep, probe, 0.0)
            high, low = halves(probe)
            sample = mm(high, x, NT) + mm(low, x, NT)
            s_ref[t] = sample
            high, low = halves(sample)
            cross = mm(high, low, NT)
            gram = mm(high, high, NT) + (cross + cross.T)
            grams.append(gram + jnp.where(diag & ~keep, 1.0, 0.0))
        inverse = inverse_factor(jnp.stack(grams))
        settle(panel)
        for spot, t in enumerate(early + late):
            a, e = tiles[t]
            high, low = halves(inverse[t])
            s_high, s_low = halves(s_ref[t])
            basis = mm(high, s_high) + (mm(high, s_low) + mm(low, s_high))
            fresh_u = (basis * tile_size**0.5).T.astype(BF16)
            x = x_ref[t]
            high, low = halves(basis)
            weights = mm(high, x) + mm(low, x)
            w_high, w_low = halves(weights)
            old_u, old_v = from_u[a, e], from_v[a, e]
            y = jnp.concatenate([old_v, top_ref[panel, 1, e]], axis=1)
            fresh_v = ((mm(y, w_high, NT) + mm(y, w_low, NT)) * tile_size**-0.5).astype(BF16)
            if a == 0:
                old_u = jnp.where(rows[a] == panel, turned_ref[e], old_u)
            if e == 0:
                old_v = jnp.where(cols[e] == panel, side_ref[a], old_v)
            active = (rows[a] > panel) & (cols[e] > panel)
            out_u_ref[a, e] = jnp.where(active, fresh_u, old_u)
            out_v_ref[a, e] = jnp.where(active, fresh_v, old_v)
            if spot == len(early) - 1 and panel + 1 < PANELS:
                launch(panel + 1)


def on_device(
    row_size, col_size, tile_u, tile_v, tile_ranks, lower_inverse, upper_inverse, row_order, sketch
):
    row_tiles, col_tiles = tile_u.shape[0], tile_u.shape[2]
    tile_size, rank_width = tile_u.shape[4], tile_u.shape[5]
    shape_four = (row_tiles, col_tiles, tile_size, rank_width)
    ranks = tile_ranks.reshape(row_tiles, col_tiles)
    keep = (jnp.arange(rank_width, dtype=jnp.int32) < ranks[:, :, None]).astype(BF16)
    u = tile_u.reshape(shape_four) * keep[:, :, None, :]
    v = tile_v.reshape(shape_four) * keep[:, :, None, :]
    tiles = row_tiles * col_tiles
    vmem = pl.BlockSpec(memory_space=pltpu.VMEM)
    tops, lefts = 2 * col_tiles * CHUNKS, 2 * row_tiles * CHUNKS
    new_u, new_v = pl.pallas_call(
        functools.partial(panels_kernel, row_size, col_size),
        out_shape=(
            jax.ShapeDtypeStruct(shape_four, BF16),
            jax.ShapeDtypeStruct(shape_four, BF16),
        ),
        in_specs=[pl.BlockSpec(memory_space=pltpu.SMEM)] + [vmem] * 6,
        out_specs=(vmem, vmem),
        scratch_shapes=[
            pltpu.VMEM((PANELS, 2, col_tiles, tile_size, rank_width), BF16),
            pltpu.VMEM((PANELS, 2, row_tiles, tile_size, rank_width), BF16),
            pltpu.VMEM((PANELS, tile_size, tile_size), BF16),
            pltpu.VMEM((col_tiles, tile_size, rank_width), BF16),
            pltpu.VMEM((row_tiles, tile_size, rank_width), BF16),
            pltpu.VMEM((tiles, tile_size, 2 * rank_width), BF16),
            pltpu.VMEM((tiles, rank_width, tile_size), F32),
            pltpu.SemaphoreType.DMA((PANELS, tops, 2)),
            pltpu.SemaphoreType.DMA((PANELS, tops)),
            pltpu.SemaphoreType.DMA((PANELS, lefts, 2)),
            pltpu.SemaphoreType.DMA((PANELS, lefts)),
        ],
        compiler_params=pltpu.CompilerParams(collective_id=0, has_side_effects=True),
        name="panels",
    )(ranks.reshape(-1), u, v, lower_inverse, upper_inverse, row_order, sketch)
    return new_u.reshape(tile_u.shape), new_v.reshape(tile_v.shape)


def solution(mesh):
    tile_spec = P(None, "row", None, "col", None, None)
    return jax.shard_map(
        functools.partial(on_device, mesh.shape["row"], mesh.shape["col"]),
        mesh=mesh,
        in_specs=(tile_spec, tile_spec, P(None, "row", None, "col"), P(), P(), P(), P()),
        out_specs=(tile_spec, tile_spec),
        check_vma=False,
    )
```

time: 300 us -> 94.1 us (0.31)
  the two profiles are of different devices: /device:TPU:28 before, /device:TPU:26 now
where the time goes in v2:
time: 94.1 us; the launch traced here: 93.9 us
  Pallas kernels  86.1 us (91%)
  local copies, waits for them, and re-layouts  4.44 us (5%)
  other arithmetic  2.69 us (3%)
    pallas_call x1, Pallas kernels, on_device(): pl.pallas_call(functools.partial(panels_kernel, row_size, col_size), out_...  86.1 us
    unnamed x7, local copies, waits for them, and re-layouts  3.78 us
    mul x1, other arithmetic, on_device(): v = tile_v.reshape(shape_four) * keep[:, :, None, :]  2.61 us

profile of v2, /device:TPU:26, one launch (start us, length us, event | category | flops | bytes accessed | tf_op | source)
XLA Modules:
  0.0 93.9 jit_solution(10799779686947771373)
XLA Ops:
  0.6 0.0 copy-start.1
  0.6 0.7 copy-done.1
  1.3 0.1 copy.14
  1.4 0.1 compare_convert_fusion
  1.5 0.1 copy.13
  1.6 0.6 reshape_reshape.3.ranks_ref
  2.1 2.6 %bitcast_multiply_fusion = (bf16[3,2,512,128]{3,2,1,0:T(8,128)(2,1)}, bf16[3,2,512,128]{3,2,1,0:T(8,128)(2,1)}) fusion(bf16[3,1,2,1,512,128]{5,4,3,2,1,0:T(8,128)(2,1)} %param.8, bf16[3,2,128]{2,1,0:T(2,128)(2,1)S(1)} %compare_convert_fusion, bf16[3,1,2,1,512,128]{5,4,3,2,1,0:T(8,128)(2,1)} %param.7), kind=kLoop, calls=%fused_computation | loop fusion | flops 786432 | bytes 3147264 | tf_op jit(solution)/shard_map/mul | solution.py:319
  4.8 86.1 %panels.1 = (bf16[3,2,512,128]{3,2,1,0:T(8,128)(2,1)}, bf16[3,2,512,128]{3,2,1,0:T(8,128)(2,1)}) custom-call(s32[6]{0:T(128)} %reshape_reshape.3.ranks_ref, bf16[3,2,512,128]{3,2,1,0:T(8,128)(2,1)} %get-tuple-element.11.u_ref, bf16[3,2,512,128]{3,2,1,0:T(8,128)(2,1)} %get-tuple-element.10.v_ref, bf16[2,512,512]{2,1,0:T(8,128)(2,1)} %lower_ref.1, ...), custom_call_target="tpu_custom_call" | custom-call | tf_op jit(solution)/shard_map/panels/pallas_call | solution.py:323
  90.8 0.0 copy-start
  90.8 2.1 %copy.19 = bf16[3,1,2,1,512,128]{5,4,3,2,1,0:T(8,128)(2,1)} copy(bf16[3,1,2,1,512,128]{5,4,3,2,1,0:T(8,128)(2,1)} %bitcast.14) | data formatting | bytes 1572864
  93.0 0.0 copy-done
  93.0 0.9 copy.20
Async XLA Ops:
  0.6 0.7 copy-start.1
  90.8 2.1 %copy-start = (bf16[3,2,512,128]{3,2,1,0:T(8,128)(2,1)S(1)}, bf16[3,2,512,128]{3,2,1,0:T(8,128)(2,1)}, u32[]{:S(2)}) copy-start(bf16[3,2,512,128]{3,2,1,0:T(8,128)(2,1)} %get-tuple-element.5) | copy-start | bytes 2359300

commit v3 on v2

--- a/solution.py
+++ b/solution.py
@@ -80,23 +80,31 @@
 
 
 class Tree:
-    def __init__(self, axis, size, root):
+    def __init__(self, axis, size, root, crossed=False):
         place = lax.axis_index(axis)
         self.axis = axis
         self.pair = place + 1 - 2 * lax.rem(place, 2)
-        self.chain = lax.rem(place, 2) == root
         self.is_root = place == root
-        self.has_next = self.chain & (place + 2 < size)
         self.next = jnp.minimum(place + 2, size - 1)
-        self.parent = jnp.where(self.chain, jnp.maximum(place - 2, 0), self.pair)
-        self.place = place
+        before = jnp.maximum(place - 2, 0)
+        self.home = lax.rem(place, 2) == root
+        if crossed:
+            self.chain = ~self.home
+            self.has_next = self.chain & (place + 2 < size)
+            self.has_pair = (self.chain & (place >= 2)) | self.is_root
+            self.parent = jnp.where(self.chain & (place >= 2), before, self.pair)
+        else:
+            self.chain = self.home
+            self.has_next = self.chain & (place + 2 < size)
+            self.has_pair = self.chain
+            self.parent = jnp.where(self.chain, before, self.pair)
 
     def greet(self, barrier):
         @pl.when(~self.is_root)
         def _():
             self.signal(barrier, self.parent)
 
-        @pl.when(self.chain)
+        @pl.when(self.has_pair)
         def _():
             self.signal(barrier, self.pair)
 
@@ -112,7 +120,7 @@
     def met(self):
         return (
             (~self.is_root).astype(jnp.int32)
-            + self.chain.astype(jnp.int32)
+            + self.has_pair.astype(jnp.int32)
             + self.has_next.astype(jnp.int32)
         )
 
@@ -126,12 +134,13 @@
             device_id_type=pl.DeviceIdType.MESH,
         )
 
-    def send(self, source, target, sends, recv, c):
+    def send_next(self, source, target, sends, recv, c):
         @pl.when(self.has_next)
         def _():
             self.copy(source, target, sends.at[c, 0], recv.at[c], self.next).start()
 
-        @pl.when(self.chain)
+    def send_pair(self, source, target, sends, recv, c):
+        @pl.when(self.has_pair)
         def _():
             self.copy(source, target, sends.at[c, 1], recv.at[c], self.pair).start()
 
@@ -140,7 +149,7 @@
         def _():
             self.copy(target, target, sends.at[c, 0], recv.at[c], self.next).wait_send()
 
-        @pl.when(self.chain)
+        @pl.when(self.has_pair)
         def _():
             self.copy(target, target, sends.at[c, 1], recv.at[c], self.pair).wait_send()
 
@@ -180,11 +189,12 @@
     late = [t for t, (a, e) in enumerate(tiles) if a > 0 and e > 0]
     piece = tile_size // CHUNKS
     row_trees = [Tree("row", row_size, panel) for panel in range(PANELS)]
+    cross_trees = [Tree("row", row_size, panel, True) for panel in range(PANELS)]
     col_trees = [Tree("col", col_size, panel) for panel in range(PANELS)]
 
     barrier = pltpu.get_barrier_semaphore()
     met = 0
-    for tree in row_trees + col_trees:
+    for tree in row_trees + cross_trees + col_trees:
         tree.greet(barrier)
         met = met + tree.met()
     pl.semaphore_wait(barrier, met)
@@ -199,19 +209,35 @@
                     top.append((ref.at[0, e, part], top_ref.at[panel, which, e, part]))
                 for a in range(row_tiles):
                     left.append((ref.at[a, 0, part], left_ref.at[panel, which, a, part]))
-        return [
-            (row_trees[panel], top, top_send.at[panel], top_recv.at[panel]),
-            (col_trees[panel], left, left_send.at[panel], left_recv.at[panel]),
-        ]
+        straight, crossed, side = [], [], []
+        for c, (source, target) in enumerate(top):
+            sems = (top_send.at[panel], top_recv.at[panel], c)
+            if c % 2 == 0:
+                straight.append((row_trees[panel], source, target, sems))
+            else:
+                crossed.append((cross_trees[panel], source, target, sems))
+        for c, (source, target) in enumerate(left):
+            sems = (left_send.at[panel], left_recv.at[panel], c)
+            side.append((col_trees[panel], source, target, sems))
+        return straight, crossed, side
 
     def launch(panel):
         u_from, v_from = (u_ref, v_ref) if panel == 0 else (out_u_ref, out_v_ref)
-        for tree, pieces, sends, recv in flows(panel):
-
-            @pl.when(tree.is_root)
-            def _():
-                for c, (source, target) in enumerate(pieces):
-                    tree.send(source, target, sends, recv, c)
+        straight, crossed, side = flows(panel)
+
+        @pl.when(row_trees[panel].is_root)
+        def _():
+            for one, other in zip(straight, crossed):
+                one[0].send_next(one[1], one[2], *one[3])
+                other[0].send_pair(other[1], other[2], *other[3])
+            for tree, source, target, sems in straight:
+                tree.send_pair(source, target, *sems)
+
+        @pl.when(col_trees[panel].is_root)
+        def _():
+            for tree, source, target, sems in side:
+                tree.send_next(source, target, *sems)
+                tree.send_pair(source, target, *sems)
 
         @pl.when(row_trees[panel].is_root)
         def _():
@@ -224,24 +250,35 @@
             left_ref[panel, 1] = v_from[:, 0]
 
     def relay(panel):
-        pending = [
-            (c / len(pieces), which, c)
-            for which, (_, pieces, _, _) in enumerate(flows(panel))
-            for c in range(len(pieces))
-        ]
-        for _, which, c in sorted(pending):
-            tree, pieces, sends, recv = flows(panel)[which]
-            target = pieces[c][1]
-
-            @pl.when(~tree.is_root)
-            def _():
-                tree.received(target, sends, recv, c)
-                tree.send(target, target, sends, recv, c)
+        straight, crossed, side = flows(panel)
+
+        def follow(first, last):
+            pending = [
+                (c / len(pieces), which, piece_of)
+                for which, pieces in enumerate((first, side))
+                for c, piece_of in enumerate(pieces)
+            ]
+            pending.sort(key=lambda item: item[:2])
+            for tree, _, target, sems in [item[2] for item in pending] + last:
+
+                @pl.when(~tree.is_root)
+                def _():
+                    tree.received(target, *sems)
+                    tree.send_next(target, target, *sems)
+                    tree.send_pair(target, target, *sems)
+
+        @pl.when(row_trees[panel].home)
+        def _():
+            follow(straight, crossed)
+
+        @pl.when(~row_trees[panel].home)
+        def _():
+            follow(crossed, straight)
 
     def settle(panel):
-        for tree, pieces, sends, recv in flows(panel):
-            for c, (_, target) in enumerate(pieces):
-                tree.sent(target, sends, recv, c)
+        for pieces in flows(panel):
+            for tree, _, target, sems in pieces:
+                tree.sent(target, *sems)
 
     launch(0)
     place = lax.broadcasted_iota(jnp.int32, (tile_size, tile_size), 0)
@@ -290,12 +327,10 @@
             basis = mm(high, s_high) + (mm(high, s_low) + mm(low, s_high))
             fresh_u = (basis * tile_size**0.5).T.astype(BF16)
             x = x_ref[t]
-            high, low = halves(basis)
-            weights = mm(high, x) + mm(low, x)
-            w_high, w_low = halves(weights)
+            weights = mm(basis.astype(BF16), x).astype(BF16)
             old_u, old_v = from_u[a, e], from_v[a, e]
             y = jnp.concatenate([old_v, top_ref[panel, 1, e]], axis=1)
-            fresh_v = ((mm(y, w_high, NT) + mm(y, w_low, NT)) * tile_size**-0.5).astype(BF16)
+            fresh_v = (mm(y, weights, NT) * tile_size**-0.5).astype(BF16)
             if a == 0:
                 old_u = jnp.where(rows[a] == panel, turned_ref[e], old_u)
             if e == 0:

time: 94.1 us -> 85.1 us (0.904)
  the two profiles are of different devices: /device:TPU:26 before, /device:TPU:28 now
where the time goes in v3:
time: 85.1 us; the launch traced here: 85 us
  Pallas kernels  77.2 us (91%)
  local copies, waits for them, and re-layouts  4.44 us (5%)
  other arithmetic  2.69 us (3%)
    pallas_call x1, Pallas kernels, on_device(): pl.pallas_call(functools.partial(panels_kernel, row_size, col_size), out_...  77.2 us
    unnamed x7, local copies, waits for them, and re-layouts  3.78 us
    mul x1, other arithmetic, on_device(): v = tile_v.reshape(shape_four) * keep[:, :, None, :]  2.61 us

profile of v3, /device:TPU:28, one launch (start us, length us, event | category | flops | bytes accessed | tf_op | source)
XLA Modules:
  0.0 85.0 jit_solution(3024445242900180067)
XLA Ops:
  0.6 0.0 copy-start.1
  0.6 0.7 copy-done.1
  1.3 0.1 copy.14
  1.4 0.1 compare_convert_fusion
  1.5 0.1 copy.13
  1.6 0.6 reshape_reshape.3.ranks_ref
  2.1 2.6 %bitcast_multiply_fusion = (bf16[3,2,512,128]{3,2,1,0:T(8,128)(2,1)}, bf16[3,2,512,128]{3,2,1,0:T(8,128)(2,1)}) fusion(bf16[3,1,2,1,512,128]{5,4,3,2,1,0:T(8,128)(2,1)} %param.8, bf16[3,2,128]{2,1,0:T(2,128)(2,1)S(1)} %compare_convert_fusion, bf16[3,1,2,1,512,128]{5,4,3,2,1,0:T(8,128)(2,1)} %param.7), kind=kLoop, calls=%fused_computation | loop fusion | flops 786432 | bytes 3147264 | tf_op jit(solution)/shard_map/mul | solution.py:354
  4.8 77.2 %panels.1 = (bf16[3,2,512,128]{3,2,1,0:T(8,128)(2,1)}, bf16[3,2,512,128]{3,2,1,0:T(8,128)(2,1)}) custom-call(s32[6]{0:T(128)} %reshape_reshape.3.ranks_ref, bf16[3,2,512,128]{3,2,1,0:T(8,128)(2,1)} %get-tuple-element.11.u_ref, bf16[3,2,512,128]{3,2,1,0:T(8,128)(2,1)} %get-tuple-element.10.v_ref, bf16[2,512,512]{2,1,0:T(8,128)(2,1)} %lower_ref.1, ...), custom_call_target="tpu_custom_call" | custom-call | tf_op jit(solution)/shard_map/panels/pallas_call | solution.py:358
  81.9 0.0 copy-start
  81.9 2.1 %copy.19 = bf16[3,1,2,1,512,128]{5,4,3,2,1,0:T(8,128)(2,1)} copy(bf16[3,1,2,1,512,128]{5,4,3,2,1,0:T(8,128)(2,1)} %bitcast.14) | data formatting | bytes 1572864
  84.1 0.0 copy-done
  84.1 0.9 %copy.20 = bf16[3,1,2,1,512,128]{5,4,3,2,1,0:T(8,128)(2,1)} copy(bf16[3,1,2,1,512,128]{5,4,3,2,1,0:T(8,128)(2,1)S(1)} %bitcast.13) | data formatting | bytes 1572864
Async XLA Ops:
  0.6 0.7 copy-start.1
  81.9 2.1 %copy-start = (bf16[3,2,512,128]{3,2,1,0:T(8,128)(2,1)S(1)}, bf16[3,2,512,128]{3,2,1,0:T(8,128)(2,1)}, u32[]{:S(2)}) copy-start(bf16[3,2,512,128]{3,2,1,0:T(8,128)(2,1)} %get-tuple-element.5) | copy-start | bytes 2359300

commit v4 on v3

--- a/solution.py
+++ b/solution.py
@@ -39,20 +39,29 @@
         groups = [
             below[:, at : at + GROUP, :] for at in range(0, BLOCK, GROUP)
         ]
-        scales = []
-        for step in range(BLOCK):
+        for step in range(0, BLOCK, 2):
             pivot = first + step
             home, line = divmod(step, GROUP)
             own = groups[home]
-            row = own[:, line : line + 1, :]
-            inverse = 1.0 / row[:, :, pivot : pivot + 1]
-            at_pivot = lane == pivot
-            turned = jnp.where(at_pivot, 1.0, row) * inverse
+            one, two = own[:, line : line + 1, :], own[:, line + 1 : line + 2, :]
+            at_one, at_two = lane == pivot, lane == pivot + 1
+            lead = two[:, :, pivot : pivot + 1]
+            inverse = 1.0 / one[:, :, pivot : pivot + 1]
+            ratio = one[:, :, pivot + 1 : pivot + 2] * inverse
+            inverse_two = 1.0 / (two[:, :, pivot + 1 : pivot + 2] - lead * ratio)
+            turned = jnp.where(at_one, 1.0, one) * inverse
+            two = jnp.where(at_one, 0.0, two) - lead * turned
+            turned_two = jnp.where(at_two, 1.0, two) * inverse_two
             for g in range(home, BLOCK // GROUP):
                 value = groups[g]
                 column = value[:, :, pivot : pivot + 1]
-                fresh = jnp.where(at_pivot, 0.0, value) - column * turned
-                groups[g] = jnp.where(sub > line, fresh, value) if g == home else fresh
+                column_two = value[:, :, pivot + 1 : pivot + 2] - column * ratio
+                middle = jnp.where(at_one, 0.0, value) - column * turned
+                fresh = jnp.where(at_two, 0.0, middle) - column_two * turned_two
+                if g == home:
+                    middle = jnp.where(sub > line, middle, value)
+                    fresh = jnp.where(sub > line + 1, fresh, middle)
+                groups[g] = fresh
         block = jnp.concatenate(groups, axis=1)
         row_id = first + lax.broadcasted_iota(jnp.int32, (1, BLOCK, 1), 1)
         diagonal = jnp.sum(jnp.where(lane == row_id, block, 0.0), axis=2, keepdims=True)

time: 85.1 us -> 102 us (1.20)
  Pallas kernels: 77.2 us -> 94.5 us
    pallas_call x1, Pallas kernels: 77.2 us -> 94.5 us  [on_device(): pl.pallas_call(functools.partial(panels_kernel, row_size, col_size), out_...]
where the time goes in v4:
time: 102 us
  Pallas kernels  94.5 us (93%)
  local copies, waits for them, and re-layouts  4.44 us (4%)
  other arithmetic  2.69 us (3%)
    pallas_call x1, Pallas kernels, on_device(): pl.pallas_call(functools.partial(panels_kernel, row_size, col_size), out_...  94.5 us
    unnamed x7, local copies, waits for them, and re-layouts  3.78 us
    mul x1, other arithmetic, on_device(): v = tile_v.reshape(shape_four) * keep[:, :, None, :]  2.61 us

profile of v4, /device:TPU:28, one launch (start us, length us, event | category | flops | bytes accessed | tf_op | source)
XLA Modules:
  0.0 102.2 jit_solution(7281348354533860937)
XLA Ops:
  0.6 0.0 copy-start.1
  0.6 0.7 copy-done.1
  1.3 0.1 copy.14
  1.4 0.1 compare_convert_fusion
  1.5 0.1 copy.13
  1.6 0.6 reshape_reshape.3.ranks_ref
  2.1 2.6 %bitcast_multiply_fusion = (bf16[3,2,512,128]{3,2,1,0:T(8,128)(2,1)}, bf16[3,2,512,128]{3,2,1,0:T(8,128)(2,1)}) fusion(bf16[3,1,2,1,512,128]{5,4,3,2,1,0:T(8,128)(2,1)} %param.8, bf16[3,2,128]{2,1,0:T(2,128)(2,1)S(1)} %compare_convert_fusion, bf16[3,1,2,1,512,128]{5,4,3,2,1,0:T(8,128)(2,1)} %param.7), kind=kLoop, calls=%fused_computation | loop fusion | flops 786432 | bytes 3147264 | tf_op jit(solution)/shard_map/mul | solution.py:363
  4.8 94.5 %panels.1 = (bf16[3,2,512,128]{3,2,1,0:T(8,128)(2,1)}, bf16[3,2,512,128]{3,2,1,0:T(8,128)(2,1)}) custom-call(s32[6]{0:T(128)} %reshape_reshape.3.ranks_ref, bf16[3,2,512,128]{3,2,1,0:T(8,128)(2,1)} %get-tuple-element.11.u_ref, bf16[3,2,512,128]{3,2,1,0:T(8,128)(2,1)} %get-tuple-element.10.v_ref, bf16[2,512,512]{2,1,0:T(8,128)(2,1)} %lower_ref.1, ...), custom_call_target="tpu_custom_call" | custom-call | tf_op jit(solution)/shard_map/panels/pallas_call | solution.py:367
  99.2 0.0 copy-start
  99.2 2.1 %copy.19 = bf16[3,1,2,1,512,128]{5,4,3,2,1,0:T(8,128)(2,1)} copy(bf16[3,1,2,1,512,128]{5,4,3,2,1,0:T(8,128)(2,1)} %bitcast.14) | data formatting | bytes 1572864
  101.4 0.0 copy-done
  101.4 0.9 copy.20
Async XLA Ops:
  0.6 0.7 copy-start.1
  99.2 2.1 %copy-start = (bf16[3,2,512,128]{3,2,1,0:T(8,128)(2,1)S(1)}, bf16[3,2,512,128]{3,2,1,0:T(8,128)(2,1)}, u32[]{:S(2)}) copy-start(bf16[3,2,512,128]{3,2,1,0:T(8,128)(2,1)} %get-tuple-element.5) | copy-start | bytes 2359300
